TPU v7x, 256 devices: a whole 4x4x8 slice. The times are simulated.
256 devices in a mesh: tm: 16 (over z, core), tok: 16 (over x, y).
Axes of the slice: x: 4, y: 4, z: 8, core: 2. Of those that a mesh axis runs over, the one named last changes fastest.
Arguments:
- queries: bfloat16 [32, 2048, 1024], P('tm', 'tok'), may hold values from -6 to 6
- keys: bfloat16 [32, 2048, 1024], P('tm', 'tok'), may hold values from -6 to 6
- values: bfloat16 [32, 2048, 1024], P('tm', 'tok'), may hold values from -6 to 6
- epi_dev: int32 [32, 6], replicated, may hold values from 0 to 15, all different within a row; in each aligned block of 2 rows (0 to 1, 2 to 3, ...) at most 2 rows name the same one
- epi_frame: int32 [32, 6], replicated, may hold values from 0 to 1
- epi_block: int32 [32, 6], replicated, may hold values from 0 to 15
- valid: int32 [32, 6], replicated, may hold values 0 or 1
- ref_local: int32 [4], replicated, may hold values from 0 to 7
Outputs:
- attended: bfloat16 [32, 2048, 1024], P('tm', 'tok')
Inputs may be any that keep to these rules, and one draw needn't show every extreme that they name: `epi_dev`: the 6 values of one frame differ. Among the frames of one index of tm (aligned blocks of 2 frames), no value is named by more than 2 entries, a bound that some block reaches.
All inputs are finite; a program needn't handle non-finite values.
Results may differ from a plain program's by a relative error of at most 0.0032.
Values may be sent and summed in bfloat16 or wider, within the bound.
A program may use at most 128 MiB of HBM per device.

v0:
```python
import math

import jax
import jax.numpy as jnp
from jax import lax
from jax.sharding import PartitionSpec as P

HEADS = 16
HEAD_DIM = 64
BLOCK = 128
FRAMES_DEV = 2
ENTRIES = 6
SPAN = 4


def attend_frame(query_slab, key_set, value_set, live_mask, local_heads):
    row_count = query_slab.shape[0]
    block_rows = math.gcd(row_count, 1024)
    query_blocks = query_slab.reshape(row_count // block_rows, block_rows, local_heads, HEAD_DIM)
    key_heads = key_set.reshape(key_set.shape[0], local_heads, HEAD_DIM)
    value_heads = value_set.reshape(value_set.shape[0], local_heads, HEAD_DIM)
    score_scale = HEAD_DIM ** (-0.5)

    def per_block(query_block):
        scores = (
            jnp.einsum("qhd,khd->hqk", query_block, key_heads, preferred_element_type=jnp.float32)
            * score_scale
        )
        scores = jnp.where(live_mask > 0, scores, -1e30)
        row_max = jnp.max(scores, axis=-1, keepdims=True)
        weights = jnp.exp(scores - row_max) * live_mask
        weight_sum = jnp.sum(weights, axis=-1)
        attended = jnp.einsum(
            "hqk,khd->qhd",
            weights.astype(jnp.bfloat16),
            value_heads,
            preferred_element_type=jnp.float32,
        )
        attended = attended / jnp.transpose(weight_sum)[:, :, None]
        return attended.astype(jnp.bfloat16).reshape(block_rows, local_heads * HEAD_DIM)

    return lax.map(per_block, query_blocks).reshape(row_count, local_heads * HEAD_DIM)


def shards(queries, keys, values, epi_dev, epi_frame, epi_block, valid, ref_local):
    local_heads = HEADS // lax.axis_size("tok")
    head_q, head_k, head_v = (
        lax.all_to_all(queries, "tok", split_axis=2, concat_axis=1, tiled=True),
        lax.all_to_all(keys, "tok", split_axis=2, concat_axis=1, tiled=True),
        lax.all_to_all(values, "tok", split_axis=2, concat_axis=1, tiled=True),
    )
    frame_len = head_q.shape[1]
    slab_width = head_q.shape[2]
    my_index = lax.axis_index("tm")
    group_frames = SPAN * FRAMES_DEV
    first_frame = my_index * FRAMES_DEV
    source = epi_dev * FRAMES_DEV + epi_frame
    my_source = lax.dynamic_slice_in_dim(source, first_frame, FRAMES_DEV, 0)
    my_block = lax.dynamic_slice_in_dim(epi_block, first_frame, FRAMES_DEV, 0)
    my_valid = lax.dynamic_slice_in_dim(valid, first_frame, FRAMES_DEV, 0)
    my_group = my_index // SPAN
    ref_frame = my_group * group_frames + lax.dynamic_index_in_dim(
        ref_local, my_group, 0, keepdims=False
    )

    def collect(carry, piece):
        epi_keys, epi_values, ref_keys, ref_values = carry
        piece_keys, piece_values = piece
        piece_len = piece_keys.shape[0]

        def pick_block(frame_index, block_index):
            offset = frame_index
            inside = (offset >= 0) & (offset < piece_len)
            offset = jnp.clip(offset, 0, piece_len - 1)
            corner = (offset, block_index * BLOCK, 0)
            got_keys = lax.dynamic_slice(piece_keys, corner, (1, BLOCK, slab_width))[0]
            got_values = lax.dynamic_slice(piece_values, corner, (1, BLOCK, slab_width))[0]
            return (inside, got_keys, got_values)

        inside, new_keys, new_values = jax.vmap(jax.vmap(pick_block))(my_source, my_block)
        epi_keys = jnp.where(inside[:, :, None, None], new_keys, epi_keys)
        epi_values = jnp.where(inside[:, :, None, None], new_values, epi_values)
        ref_offset = ref_frame
        ref_inside = (ref_offset >= 0) & (ref_offset < piece_len)
        ref_offset = jnp.clip(ref_offset, 0, piece_len - 1)
        ref_keys = jnp.where(
            ref_inside,
            lax.dynamic_index_in_dim(piece_keys, ref_offset, 0, keepdims=False),
            ref_keys,
        )
        ref_values = jnp.where(
            ref_inside,
            lax.dynamic_index_in_dim(piece_values, ref_offset, 0, keepdims=False),
            ref_values,
        )
        return (epi_keys, epi_values, ref_keys, ref_values)

    epi_empty = jnp.zeros((FRAMES_DEV, ENTRIES, BLOCK, slab_width), jnp.bfloat16)
    ref_empty = jnp.zeros((frame_len, slab_width), jnp.bfloat16)
    epi_keys, epi_values, ref_keys, ref_values = collect(
        (epi_empty, epi_empty, ref_empty, ref_empty),
        (
            lax.all_gather(head_k, "tm", axis=0, tiled=True),
            lax.all_gather(head_v, "tm", axis=0, tiled=True),
        ),
    )
    live_epi = my_valid.astype(jnp.float32)

    def one_frame(packed):
        query_slab, key_slab, value_slab, extra_keys, extra_values, extra_live = packed
        key_set = jnp.concatenate(
            [key_slab, ref_keys, extra_keys.reshape(ENTRIES * BLOCK, slab_width)], 0
        )
        value_set = jnp.concatenate(
            [value_slab, ref_values, extra_values.reshape(ENTRIES * BLOCK, slab_width)], 0
        )
        live_mask = jnp.concatenate(
            [jnp.ones((2 * frame_len,), jnp.float32), jnp.repeat(extra_live, BLOCK)]
        )
        return attend_frame(query_slab, key_set, value_set, live_mask, local_heads)

    attended = lax.map(one_frame, (head_q, head_k, head_v, epi_keys, epi_values, live_epi))
    return lax.all_to_all(attended, "tok", split_axis=1, concat_axis=2, tiled=True)


def solution(mesh):
    return jax.shard_map(
        shards,
        mesh=mesh,
        in_specs=(
            P("tm", "tok", None),
            P("tm", "tok", None),
            P("tm", "tok", None),
            P(),
            P(),
            P(),
            P(),
            P(),
        ),
        out_specs=P("tm", "tok", None),
        check_vma=False,
    )
```

profile of v0, /device:TPU:24, one launch (start us, length us, event | category | flops | bytes accessed | tf_op | source)
XLA Modules:
  0.0 324.3 jit_solution(2710502964879535446)
XLA Ops:
  6.5 1.3 copy.89
  7.8 15.9 %all_to_all.72 = bf16[2,128,1024]{1,0,2:T(2,128)(2,1)S(1)} all-to-all(bf16[2,128,1024]{1,0,2:T(2,128)(2,1)S(1)} %copy.89), channel_id=1, replica_groups=mesh['tm'=16,'tok'=16] {'tok'}, dimensions={2} | all-to-all | bytes 1048576 | tf_op jit(solution)/shard_map/all_to_all | solution.py:49
  23.8 1.0 copy.127
  24.9 1.3 copy.97
  26.2 13.6 %all_to_all.73 = bf16[2,128,1024]{1,0,2:T(2,128)(2,1)S(1)} all-to-all(bf16[2,128,1024]{1,0,2:T(2,128)(2,1)S(1)} %copy.97), channel_id=1, replica_groups=mesh['tm'=16,'tok'=16] {'tok'}, dimensions={2} | all-to-all | bytes 1048576 | tf_op jit(solution)/shard_map/all_to_all | solution.py:50
  39.9 0.9 copy.126
  40.8 2.0 copy.86
  42.9 6.1 %all-to-all-start = ((bf16[2,128,1024]{1,0,2:T(2,128)(2,1)}), bf16[2,128,1024]{1,0,2:T(2,128)(2,1)S(1)}, u32[]{:S(2)}, u32[]{:S(2)}) async-start(bf16[2,128,1024]{1,0,2:T(2,128)(2,1)} %copy.86), calls=%async_computation | async-start | bytes 1048576 | tf_op jit(solution)/shard_map/all_to_all | solution.py:48
  48.9 1.3 dynamic_slice.47
  51.5 0.8 fusion.31
  52.8 3.7 %all-to-all-done = bf16[2,128,1024]{1,0,2:T(2,128)(2,1)S(1)} async-done(((bf16[2,128,1024]{1,0,2:T(2,128)(2,1)}), bf16[2,128,1024]{1,0,2:T(2,128)(2,1)S(1)}, u32[]{:S(2)}, u32[]{:S(2)}) %all-to-all-start) | async-done | bytes 524320 | tf_op jit(solution)/shard_map/all_to_all | solution.py:48
  56.5 0.9 copy.128
  57.5 24.9 %all-gather.3.cloned.1.call-done = bf16[32,2048,64]{1,2,0:T(8,128)(2,1)} async-done(((bf16[2,2048,64]{1,2,0:T(8,128)(2,1)}), bf16[32,2048,64]{1,2,0:T(8,128)(2,1)}) %all-gather.3.cloned.1.call-update) | async-done | bytes 8388624 | tf_op jit(solution)/shard_map/all_gather | solution.py:103
  82.4 23.9 %copy.94 = bf16[32,2048,64]{2,0,1:T(8,128)(2,1)} copy(bf16[32,2048,64]{1,2,0:T(8,128)(2,1)} %all-gather.3.cloned.1.call-done) | data formatting | bytes 16777216 | tf_op jit(solution)/shard_map/all_gather | solution.py:103
  106.4 2.8 gather_fusion
  109.5 29.1 %all-gather.5.cloned.1.call-done = bf16[32,2048,64]{1,2,0:T(8,128)(2,1)} async-done(((bf16[2,2048,64]{1,2,0:T(8,128)(2,1)}), bf16[32,2048,64]{1,2,0:T(8,128)(2,1)}) %all-gather.5.cloned.1.call-update) | async-done | bytes 8388624 | tf_op jit(solution)/shard_map/all_gather | solution.py:104
  138.7 23.9 %copy.100 = bf16[32,2048,64]{2,0,1:T(8,128)(2,1)} copy(bf16[32,2048,64]{1,2,0:T(8,128)(2,1)} %all-gather.5.cloned.1.call-done) | data formatting | bytes 16777216 | tf_op jit(solution)/shard_map/all_gather | solution.py:104
  162.6 2.7 gather_fusion.1
  165.7 0.9 broadcast_select_fusion
  166.5 1.0 select_bitcast_fusion
  167.5 1.0 select_bitcast_fusion.1
  168.5 126.6 %while.21 = (s32[]{:T(128)}, bf16[2,2048,64]{2,1,0:T(8,128)(2,1)}, bf16[2,2048,64]{1,2,0:T(8,128)(2,1)}, bf16[2,2048,64]{1,2,0:T(8,128)(2,1)S(1)}, bf16[2,6,128,...) while((s32[]{:T(128)}, bf16[2,2048,64]{2,1,0:T(8,128)(2,1)}, ...), condition=%wide.region_5.6_spmd, body=%wide.region_0.5_spmd.sunk | while | flops 1343687424 | bytes 69004664 | solution.py:122
  168.7 0.9 constant_dynamic-slice_fusion.9
  169.7 0.9 constant_dynamic-slice_fusion.10
  170.9 1.0 constant_dynamic-slice_fusion.8
  172.2 58.6 %while.22 = (s32[]{:T(128)}, bf16[2,1024,64]{1,2,0:T(8,128)(2,1)S(1)}, f32[4864]{0:T(1024)S(1)}, bf16[2,1024,1,64]{1,3,2,0:T(8,128)(2,1)S(1)}, bf16[4864,1,64]{0...) while((s32[]{:T(128)}, bf16[2,1024,64]{1,2,0:T(8,128)(2,1)S(1)}, f32[4864]{0:T(1024)S(1)}, ...), condition=%wide.region_4.4_spmd, body=%wide.region_1.3_spmd.sunk | while | flops 1339951872 | bytes 61376084 | solution.py:42
  172.2 8.3 %fusion.43 = (f32[1024]{0:T(1024)S(1)}, f32[1024,4864]{1,0:T(8,128)}) fusion(pred[4864]{0:T(1024)(128)(4,1)S(1)} %broadcast_compare_fusion.2, bf16[4864,1,64]{0,2,1:T(8,128)(2,1)S(1)} %get-tuple-element.343, bf16[2,1024,1,64]{1,3,2,0:T(8,128)(2,1)S(1)} %get-tuple-element.342, s32[]{:T(128)} %get-tuple-element.332), kind=kOutput, calls=%fused_computation.4.clone.1 | convolution fusion | flops 652475392 | bytes 20685828 | tf_op jit(solution)/shard_map/while/body/eval_jaxpr/while/body/eval_jaxpr/qhd,khd->hqk/dot_general | solution.py:26
  180.5 11.7 %fusion.44 = f32[1024]{0:T(1024)S(1)} fusion(f32[1024,4864]{1,0:T(8,128)} %get-tuple-element.323, f32[4864]{0:T(1024)S(1)} %get-tuple-element.341, f32[1024]{0:T(1024)S(1)} %get-tuple-element.324, pred[4864]{0:T(1024)(128)(4,1)S(1)} %broadcast_compare_fusion.2), kind=kLoop, calls=%fused_computation.5.clone.1 | loop fusion | flops 24902656 | bytes 19955456 | tf_op jit(solution)/shard_map/while/body/eval_jaxpr/while/body/eval_jaxpr/reduce_sum | solution.py:32
  192.2 9.2 %fusion.45 = bf16[2,1024,64]{1,2,0:T(8,128)(2,1)S(1)} fusion(bf16[2,1024,64]{1,2,0:T(8,128)(2,1)S(1)} %get-tuple-element.333, s32[]{:T(128)} %get-tuple-element.332, f32[1024,4864]{1,0:T(8,128)} %get-tuple-element.323, f32[4864]{0:T(1024)S(1)} %get-tuple-element.341, f32[1024]{0:T(1024)S(1)} %get-tuple-element.324, ...), kind=kOutput, calls=%fused_computation.12.clone.1 | convolution fusion | flops 662568960 | bytes 20710404 | tf_op jit(solution)/shard_map/while/body/eval_jaxpr/while/body/eval_jaxpr/hqk,khd->qhd/dot_general | solution.py:33
  201.5 8.3 %fusion.43 = (f32[1024]{0:T(1024)S(1)}, f32[1024,4864]{1,0:T(8,128)}) fusion(pred[4864]{0:T(1024)(128)(4,1)S(1)} %broadcast_compare_fusion.2, bf16[4864,1,64]{0,2,1:T(8,128)(2,1)S(1)} %get-tuple-element.343, bf16[2,1024,1,64]{1,3,2,0:T(8,128)(2,1)S(1)} %get-tuple-element.342, s32[]{:T(128)} %get-tuple-element.332), kind=kOutput, calls=%fused_computation.4.clone.1 | convolution fusion | flops 652475392 | bytes 20685828 | tf_op jit(solution)/shard_map/while/body/eval_jaxpr/while/body/eval_jaxpr/qhd,khd->hqk/dot_general | solution.py:26
  209.8 11.7 %fusion.44 = f32[1024]{0:T(1024)S(1)} fusion(f32[1024,4864]{1,0:T(8,128)} %get-tuple-element.323, f32[4864]{0:T(1024)S(1)} %get-tuple-element.341, f32[1024]{0:T(1024)S(1)} %get-tuple-element.324, pred[4864]{0:T(1024)(128)(4,1)S(1)} %broadcast_compare_fusion.2), kind=kLoop, calls=%fused_computation.5.clone.1 | loop fusion | flops 24902656 | bytes 19955456 | tf_op jit(solution)/shard_map/while/body/eval_jaxpr/while/body/eval_jaxpr/reduce_sum | solution.py:32
  221.5 9.2 %fusion.45 = bf16[2,1024,64]{1,2,0:T(8,128)(2,1)S(1)} fusion(bf16[2,1024,64]{1,2,0:T(8,128)(2,1)S(1)} %get-tuple-element.333, s32[]{:T(128)} %get-tuple-element.332, f32[1024,4864]{1,0:T(8,128)} %get-tuple-element.323, f32[4864]{0:T(1024)S(1)} %get-tuple-element.341, f32[1024]{0:T(1024)S(1)} %get-tuple-element.324, ...), kind=kOutput, calls=%fused_computation.12.clone.1 | convolution fusion | flops 662568960 | bytes 20710404 | tf_op jit(solution)/shard_map/while/body/eval_jaxpr/while/body/eval_jaxpr/hqk,khd->qhd/dot_general | solution.py:33
  231.1 0.9 bitcast_dynamic-update-slice_fusion.2
  231.9 0.9 constant_dynamic-slice_fusion.9
  232.9 0.9 constant_dynamic-slice_fusion.10
  234.1 1.0 constant_dynamic-slice_fusion.8
  235.4 58.6 %while.22 = (s32[]{:T(128)}, bf16[2,1024,64]{1,2,0:T(8,128)(2,1)S(1)}, f32[4864]{0:T(1024)S(1)}, bf16[2,1024,1,64]{1,3,2,0:T(8,128)(2,1)S(1)}, bf16[4864,1,64]{0...) while((s32[]{:T(128)}, bf16[2,1024,64]{1,2,0:T(8,128)(2,1)S(1)}, f32[4864]{0:T(1024)S(1)}, ...), condition=%wide.region_4.4_spmd, body=%wide.region_1.3_spmd.sunk | while | flops 1339951872 | bytes 61376084 | solution.py:42
  235.4 8.3 %fusion.43 = (f32[1024]{0:T(1024)S(1)}, f32[1024,4864]{1,0:T(8,128)}) fusion(pred[4864]{0:T(1024)(128)(4,1)S(1)} %broadcast_compare_fusion.2, bf16[4864,1,64]{0,2,1:T(8,128)(2,1)S(1)} %get-tuple-element.343, bf16[2,1024,1,64]{1,3,2,0:T(8,128)(2,1)S(1)} %get-tuple-element.342, s32[]{:T(128)} %get-tuple-element.332), kind=kOutput, calls=%fused_computation.4.clone.1 | convolution fusion | flops 652475392 | bytes 20685828 | tf_op jit(solution)/shard_map/while/body/eval_jaxpr/while/body/eval_jaxpr/qhd,khd->hqk/dot_general | solution.py:26
  243.8 11.7 %fusion.44 = f32[1024]{0:T(1024)S(1)} fusion(f32[1024,4864]{1,0:T(8,128)} %get-tuple-element.323, f32[4864]{0:T(1024)S(1)} %get-tuple-element.341, f32[1024]{0:T(1024)S(1)} %get-tuple-element.324, pred[4864]{0:T(1024)(128)(4,1)S(1)} %broadcast_compare_fusion.2), kind=kLoop, calls=%fused_computation.5.clone.1 | loop fusion | flops 24902656 | bytes 19955456 | tf_op jit(solution)/shard_map/while/body/eval_jaxpr/while/body/eval_jaxpr/reduce_sum | solution.py:32
  255.5 9.2 %fusion.45 = bf16[2,1024,64]{1,2,0:T(8,128)(2,1)S(1)} fusion(bf16[2,1024,64]{1,2,0:T(8,128)(2,1)S(1)} %get-tuple-element.333, s32[]{:T(128)} %get-tuple-element.332, f32[1024,4864]{1,0:T(8,128)} %get-tuple-element.323, f32[4864]{0:T(1024)S(1)} %get-tuple-element.341, f32[1024]{0:T(1024)S(1)} %get-tuple-element.324, ...), kind=kOutput, calls=%fused_computation.12.clone.1 | convolution fusion | flops 662568960 | bytes 20710404 | tf_op jit(solution)/shard_map/while/body/eval_jaxpr/while/body/eval_jaxpr/hqk,khd->qhd/dot_general | solution.py:33
  264.7 8.3 %fusion.43 = (f32[1024]{0:T(1024)S(1)}, f32[1024,4864]{1,0:T(8,128)}) fusion(pred[4864]{0:T(1024)(128)(4,1)S(1)} %broadcast_compare_fusion.2, bf16[4864,1,64]{0,2,1:T(8,128)(2,1)S(1)} %get-tuple-element.343, bf16[2,1024,1,64]{1,3,2,0:T(8,128)(2,1)S(1)} %get-tuple-element.342, s32[]{:T(128)} %get-tuple-element.332), kind=kOutput, calls=%fused_computation.4.clone.1 | convolution fusion | flops 652475392 | bytes 20685828 | tf_op jit(solution)/shard_map/while/body/eval_jaxpr/while/body/eval_jaxpr/qhd,khd->hqk/dot_general | solution.py:26
  273.1 11.7 %fusion.44 = f32[1024]{0:T(1024)S(1)} fusion(f32[1024,4864]{1,0:T(8,128)} %get-tuple-element.323, f32[4864]{0:T(1024)S(1)} %get-tuple-element.341, f32[1024]{0:T(1024)S(1)} %get-tuple-element.324, pred[4864]{0:T(1024)(128)(4,1)S(1)} %broadcast_compare_fusion.2), kind=kLoop, calls=%fused_computation.5.clone.1 | loop fusion | flops 24902656 | bytes 19955456 | tf_op jit(solution)/shard_map/while/body/eval_jaxpr/while/body/eval_jaxpr/reduce_sum | solution.py:32
  284.8 9.2 %fusion.45 = bf16[2,1024,64]{1,2,0:T(8,128)(2,1)S(1)} fusion(bf16[2,1024,64]{1,2,0:T(8,128)(2,1)S(1)} %get-tuple-element.333, s32[]{:T(128)} %get-tuple-element.332, f32[1024,4864]{1,0:T(8,128)} %get-tuple-element.323, f32[4864]{0:T(1024)S(1)} %get-tuple-element.341, f32[1024]{0:T(1024)S(1)} %get-tuple-element.324, ...), kind=kOutput, calls=%fused_computation.12.clone.1 | convolution fusion | flops 662568960 | bytes 20710404 | tf_op jit(solution)/shard_map/while/body/eval_jaxpr/while/body/eval_jaxpr/hqk,khd->qhd/dot_general | solution.py:33
  294.3 0.9 bitcast_dynamic-update-slice_fusion.2
  295.2 2.8 copy.129
  298.7 16.3 %all_to_all.74 = bf16[16,2,8192]{2,1,0:T(2,128)(2,1)S(1)} all-to-all(bf16[16,2,8192]{2,1,0:T(2,128)(2,1)S(1)} %reshape.95), channel_id=1, replica_groups=mesh['tm'=16,'tok'=16] {'tok'}, dimensions={0} | all-to-all | bytes 1048576 | tf_op jit(solution)/shard_map/all_to_all | solution.py:123
  315.7 0.8 copy.109
  316.5 1.0 copy.107
  (55 shorter events, 5.4 us)
Async XLA Ops:
  6.5 75.9 %all-gather.3.cloned.1.call-start = ((), (), s32[]{:S(2)}) async-start(), calls=%async_computation.4 | async-start | bytes 8912896 | tf_op jit(solution)/shard_map/all_gather | solution.py:103
  24.8 113.8 %all-gather.5.cloned.1.call-start = ((), (), s32[]{:S(2)}) async-start(), calls=%async_computation.5 | async-start | bytes 8912896 | tf_op jit(solution)/shard_map/all_gather | solution.py:104
  42.9 13.6 %all-to-all-start = ((bf16[2,128,1024]{1,0,2:T(2,128)(2,1)}), bf16[2,128,1024]{1,0,2:T(2,128)(2,1)S(1)}, u32[]{:S(2)}, u32[]{:S(2)}) async-start(bf16[2,128,1024]{1,0,2:T(2,128)(2,1)} %copy.86), calls=%async_computation | async-start | bytes 1048576 | tf_op jit(solution)/shard_map/all_to_all | solution.py:48
  106.4 62.2 %copy-start = (bf16[2,16,8,8,128]{4,3,1,2,0:T(8,128)(2,1)S(1)}, bf16[2,16,8,8,128]{4,3,1,2,0:T(8,128)(2,1)}, u32[]{:S(2)}) copy-start(bf16[2,16,8,8,128]{4,3,1,2,0:T(8,128)(2,1)} %copy.127) | copy-start | bytes 1572868
  106.4 62.2 %copy-start.1 = (bf16[2,16,8,8,128]{4,3,1,2,0:T(8,128)(2,1)S(1)}, bf16[2,16,8,8,128]{4,3,1,2,0:T(8,128)(2,1)}, u32[]{:S(2)}) copy-start(bf16[2,16,8,8,128]{4,3,1,2,0:T(8,128)(2,1)} %copy.126) | copy-start | bytes 1572868
Sparse Core Ops, SparseCore 0:
  25.0 57.3 all-gather.2
  84.2 54.3 all-gather.4
where the time goes:
time: 328 us; the launch traced here: 324 us
  local copies, waits for them, and re-layouts  78.4 us (24%)
  matrix products  70.2 us (21%)
  waiting for transfers between devices  57.8 us (18%)
  other arithmetic  51.4 us (16%)
  blocking collectives  45.8 us (14%)
  between operations  14.2 us (4%)
  starting transfers between devices  6.1 us (2%)
    reduce_sum x4, other arithmetic, per_block(): weight_sum = jnp.sum(weights, axis=-1)  46.8 us
    dot_general x4, matrix products, per_block(): jnp.einsum('hqk,khd->qhd', weights.astype(jnp.bfloat16), value_heads, pre...  36.9 us
    dot_general x4, matrix products, per_block(): jnp.einsum('qhd,khd->hqk', query_block, key_heads, preferred_element_type...  33.3 us
    all_gather x1, waiting for transfers between devices, shards(): lax.all_gather(head_v, 'tm', axis=0, tiled=True)  29.1 us
    all_gather x1, waiting for transfers between devices, shards(): lax.all_gather(head_k, 'tm', axis=0, tiled=True)  24.9 us
    all_gather x1, local copies, waits for them, and re-layouts, shards(): lax.all_gather(head_k, 'tm', axis=0, tiled=True)  23.9 us
    all_gather x1, local copies, waits for them, and re-layouts, shards(): lax.all_gather(head_v, 'tm', axis=0, tiled=True)  23.9 us
    all_to_all x1, blocking collectives, shards(): lax.all_to_all(attended, 'tok', split_axis=1, concat_axis=2, tiled=True)  16.3 us
  transfers between devices with their start and end apart: 3, of which 3 were waited for; matrix products, arithmetic and copies ran while one was open for 11% of the time, Pallas kernels for 0%

commit v1 on v0

v1 whole, which is shorter than its diff:
```python
import functools
import math

import jax
import jax.numpy as jnp
from jax import lax
from jax.experimental import pallas as pl
from jax.experimental.pallas import tpu as pltpu
from jax.sharding import PartitionSpec as P

HEADS = 16
HEAD_DIM = 64
BLOCK = 128
FRAMES_DEV = 2
ENTRIES = 6
SPAN = 4
TOKENS = 2048
N = 16
TILE = 1024
TILES = TOKENS // TILE
ROWS = HEAD_DIM + 16
EPI = ENTRIES * BLOCK
QK_SCALE = HEAD_DIM**-0.5 * math.log2(math.e)
MESH = pl.DeviceIdType.MESH
BF16 = jnp.bfloat16
F32 = jnp.float32


def low_halves(a, b):
    return jnp.concatenate([a[:, :HEAD_DIM], b[:, :HEAD_DIM]], axis=1)


def high_halves(a, b):
    return jnp.concatenate([a[:, HEAD_DIM:], b[:, HEAD_DIM:]], axis=1)


def kernel(
    q_ref, k_ref, v_ref, dev_ref, frame_ref, block_ref, valid_ref, local_ref, o_ref,
    s_kv, s_q, r_kv, r_q, s_epi, r_epi, cands, cross, r_cross, k_own, v_own, k_epi, v_epi,
    q_two, acc, top, scores, s_out, r_out, send_table, recv_table,
    sem_kv, sem_q, sem_epi, sem_out, sem_ref,
):
    tm, tok = lax.axis_index("tm"), lax.axis_index("tok")
    core, pair = lax.rem(tm, 2), lax.rem(tm // 2, 2)
    partner, across = tm + 1 - 2 * core, tm + 2 - 4 * pair
    group = tm // SPAN

    def other(me, step):
        return lax.rem(me + step, N)

    def rest(fn):
        lax.fori_loop(1, N, lambda step, _: (fn(step), 0)[1], 0)

    def copy(src, dst, sems, sent, got, axis, to):
        return pltpu.make_async_remote_copy(
            src_ref=src, dst_ref=dst, send_sem=sems.at[0, sent], recv_sem=sems.at[1, got],
            device_id={axis: to}, device_id_type=MESH,
        )

    barrier = pltpu.get_barrier_semaphore()

    def greet(step):
        pl.semaphore_signal(barrier, inc=1, device_id={"tok": other(tok, step)}, device_id_type=MESH)
        pl.semaphore_signal(barrier, inc=1, device_id={"tm": other(tm, step)}, device_id_type=MESH)

    rest(greet)

    for j in range(HEADS // 2):
        lanes = slice(j * 128, (j + 1) * 128)
        for f in range(FRAMES_DEV):
            k, v = k_ref[f, :, lanes], v_ref[f, :, lanes]
            s_kv[(2 * j) * 2 + f] = low_halves(k, v)
            s_kv[(2 * j + 1) * 2 + f] = high_halves(k, v)
        q0, q1 = q_ref[0, :, lanes], q_ref[1, :, lanes]
        s_q[2 * j] = low_halves(q0, q1)
        s_q[2 * j + 1] = high_halves(q0, q1)

    pl.semaphore_wait(barrier, 2 * (N - 1))

    def kv_copy(sent, got, to):
        return copy(s_kv.at[pl.ds(to * 2, 2)], r_kv.at[pl.ds(got * 2, 2)], sem_kv, sent, got, "tok", to)

    def q_copy(sent, got, to):
        return copy(s_q.at[to], r_q.at[got], sem_q, sent, got, "tok", to)

    rest(lambda step: kv_copy(step, tok, other(tok, step)).start())
    rest(lambda step: q_copy(step, tok, other(tok, step)).start())
    r_kv[pl.ds(tok * 2, 2)] = s_kv[pl.ds(tok * 2, 2)]
    r_q[tok] = s_q[tok]

    def fill_send(d, _):
        count, first, second = jnp.int32(0), jnp.int32(0), jnp.int32(0)
        for f in range(FRAMES_DEV):
            for e in range(ENTRIES):
                row = d * FRAMES_DEV + f
                hit = jnp.where(dev_ref[row, e] == tm, 1, 0)
                place = block_ref[row, e] * 2 + frame_ref[row, e]
                first = jnp.where((hit == 1) & (count == 0), place, first)
                second = jnp.where((hit == 1) & (count == 1), place, second)
                count = count + hit
        send_table[d * 2] = first
        send_table[d * 2 + 1] = second
        return 0

    lax.fori_loop(0, N, fill_send, 0)
    names = [dev_ref[tm * FRAMES_DEV + f, e] for f in range(FRAMES_DEV) for e in range(ENTRIES)]
    for i, name in enumerate(names):
        slot = jnp.int32(0)
        for before in names[:i]:
            slot = slot + jnp.where(before == name, 1, 0)
        recv_table[i] = name * 2 + jnp.minimum(slot, 1)

    rest(lambda step: kv_copy(step, other(tok, step), other(tok, step)).wait_recv())

    local = local_ref[group]
    owner_core, owner_pair, ref_bit = lax.rem(local // 2, 2), local // 4, lax.rem(local, 2)
    for b in range(N):
        cands[core, b] = r_kv[b * 2 + ref_bit]
    swap = copy(cands.at[core], cands.at[core], sem_ref, 0, 0, "tm", partner)
    swap.start()

    def fill_epi(i, _):
        s_epi[i] = r_kv[send_table[i]]
        return 0

    lax.fori_loop(0, 2 * N, fill_epi, 0, unroll=4)

    def ones_rows(ref, width):
        ref[0:16, :] = jnp.ones((16, width), BF16)

    for f in range(3):
        ones_rows(v_own.at[f], TOKENS)

    def build_own(b, f):
        kv = r_kv[b * 2 + f]
        at = pl.ds(pl.multiple_of(b * BLOCK, BLOCK), BLOCK)
        k_own[f, at, :] = low_halves(kv, kv)
        v_own[f, 16:, at] = kv.T[HEAD_DIM:]

    def build_frame(f):
        lax.fori_loop(0, N, lambda b, _: (build_own(b, f), 0)[1], 0, unroll=4)

    build_frame(0)
    swap.wait_recv()
    half = N // 2
    cross[...] = cands[owner_core, pl.ds(core * half, half)]
    hop = copy(cross, r_cross.at[pl.ds(core * half, half)], sem_ref, 1, 1, "tm", across)
    hop.start()

    def epi_copy(sent, got, to):
        return copy(s_epi.at[pl.ds(to * 2, 2)], r_epi.at[pl.ds(got * 2, 2)], sem_epi, sent, got, "tm", to)

    rest(lambda step: epi_copy(step, tm, other(tm, step)).start())
    r_epi[pl.ds(tm * 2, 2)] = s_epi[pl.ds(tm * 2, 2)]
    build_frame(1)

    rest(lambda step: q_copy(step, other(tok, step), other(tok, step)).wait_recv())

    def build_q(b, _):
        x = r_q[b].astype(F32) * QK_SCALE
        hi = x.astype(BF16)
        lo = (x - hi.astype(F32)).astype(BF16)
        at = pl.ds(pl.multiple_of(b * BLOCK, BLOCK), BLOCK)
        q_two[0, at, :] = low_halves(hi, lo)
        q_two[1, at, :] = high_halves(hi, lo)
        return 0

    lax.fori_loop(0, N, build_q, 0, unroll=4)

    acc[...] = jnp.zeros_like(acc)
    top[...] = jnp.full_like(top, -1e30)

    def attend(f, tile, keys, values):
        rows = pl.ds(pl.multiple_of(tile * TILE, TILE), TILE)
        length = keys.shape[0]
        s = lax.dot_general(keys[...], q_two[f, rows, :], (((1,), (1,)), ((), ())), preferred_element_type=F32)
        scores[0:length, :] = s
        peak = jnp.max(jnp.max(s.reshape(length // 8, 8, TILE), axis=0), axis=0, keepdims=True)
        old = top[f, tile]
        new = jnp.maximum(old, jnp.broadcast_to(peak, (8, TILE)))
        top[f, tile] = new
        kept = acc[f, tile] * jnp.exp2(old - new)[:1]
        probs = jnp.exp2(scores[0:length, :] - new[:1]).astype(BF16)
        acc[f, tile] = kept + jnp.dot(values[...], probs, preferred_element_type=F32)

    swap_back = copy(
        r_cross.at[pl.ds(core * half, half)], r_cross.at[pl.ds(core * half, half)], sem_ref, 2, 2, "tm", partner
    )
    swap_in = copy(
        r_cross.at[pl.ds((1 - core) * half, half)], r_cross.at[pl.ds((1 - core) * half, half)],
        sem_ref, 2, 2, "tm", partner,
    )
    phase = FRAMES_DEV * TILES

    def long_step(n, _):
        @pl.when(n == TILES)
        def _():
            hop.wait_recv()
            swap_back.start()

        @pl.when(n == phase)
        def _():
            swap_in.wait_recv()
            here = owner_pair == pair

            def build_ref(b, _):
                kv = jnp.where(here, cands[owner_core, b], r_cross[b])
                at = pl.ds(pl.multiple_of(b * BLOCK, BLOCK), BLOCK)
                k_own[2, at, :] = low_halves(kv, kv)
                v_own[2, 16:, at] = kv.T[HEAD_DIM:]
                return 0

            lax.fori_loop(0, N, build_ref, 0, unroll=4)

        f, tile = lax.rem(n // TILES, FRAMES_DEV), lax.rem(n, TILES)
        which = jnp.where(n < phase, f, 2)
        attend(f, tile, k_own.at[which], v_own.at[which])
        return 0

    lax.fori_loop(0, 2 * phase, long_step, 0)

    rest(lambda step: epi_copy(step, other(tm, step), other(tm, step)).wait_recv())
    for f in range(FRAMES_DEV):
        for e in range(ENTRIES):
            kv = r_epi[recv_table[f * ENTRIES + e]]
            used = valid_ref[tm * FRAMES_DEV + f, e] > 0
            stand_in = jnp.where(used, kv, r_kv[f])
            at = slice(e * BLOCK, (e + 1) * BLOCK)
            k_epi[f, at, :] = low_halves(stand_in, stand_in)
            weight = jnp.where(used, 1.0, 0.0).astype(F32)
            v_epi[f, 0:16, at] = jnp.full((16, BLOCK), weight, F32).astype(BF16)
            v_epi[f, 16:, at] = jnp.where(used, kv, jnp.zeros_like(kv)).T[HEAD_DIM:]

    def out_copy(sent, got, to):
        return copy(s_out.at[to], r_out.at[got], sem_out, sent, got, "tok", to)

    per_tile = TILE // BLOCK

    def short_step(n, _):
        f, tile = lax.rem(n, FRAMES_DEV), lax.rem(n // FRAMES_DEV + tok // per_tile, TILES)
        attend(f, tile, k_epi.at[f], v_epi.at[f])

        @pl.when(f == FRAMES_DEV - 1)
        def _():
            both = [acc[g, tile] for g in range(FRAMES_DEV)]
            both = [x[16:] / x[:1] for x in both]
            both = jnp.concatenate(both, axis=0).astype(BF16).T
            s_out[pl.ds(tile * per_tile, per_tile)] = both.reshape(per_tile, BLOCK, 128)
            for b in range(per_tile):
                to = tile * per_tile + b

                @pl.when(to != tok)
                def _():
                    out_copy(to, tok, to).start()

        return 0

    lax.fori_loop(0, phase, short_step, 0)
    r_out[tok] = s_out[tok]
    rest(lambda step: out_copy(other(tok, step), other(tok, step), other(tok, step)).wait_recv())
    for j in range(HEADS // 2):
        lanes = slice(j * 128, (j + 1) * 128)
        a, b = r_out[2 * j], r_out[2 * j + 1]
        o_ref[0, :, lanes] = low_halves(a, b)
        o_ref[1, :, lanes] = high_halves(a, b)

    def drain(step):
        kv_copy(step, tok, other(tok, step)).wait_send()
        q_copy(step, tok, other(tok, step)).wait_send()
        epi_copy(step, tm, other(tm, step)).wait_send()
        out_copy(other(tok, step), tok, other(tok, step)).wait_send()

    rest(drain)
    swap.wait_send()
    hop.wait_send()
    swap_back.wait_send()


def attention(queries, keys, values, epi_dev, epi_frame, epi_block, valid, ref_local):
    vmem, smem = pl.BlockSpec(memory_space=pltpu.VMEM), pl.BlockSpec(memory_space=pltpu.SMEM)
    block = (BLOCK, 128)
    return pl.pallas_call(
        kernel,
        out_shape=jax.ShapeDtypeStruct(queries.shape, BF16),
        in_specs=[vmem] * 3 + [smem] * 5,
        out_specs=vmem,
        scratch_shapes=[
            pltpu.VMEM((2 * N, *block), BF16),
            pltpu.VMEM((N, *block), BF16),
            pltpu.VMEM((2 * N, *block), BF16),
            pltpu.VMEM((N, *block), BF16),
            pltpu.VMEM((2 * N, *block), BF16),
            pltpu.VMEM((2 * N, *block), BF16),
            pltpu.VMEM((2, N, *block), BF16),
            pltpu.VMEM((N // 2, *block), BF16),
            pltpu.VMEM((N, *block), BF16),
            pltpu.VMEM((3, TOKENS, 128), BF16),
            pltpu.VMEM((3, ROWS, TOKENS), BF16),
            pltpu.VMEM((FRAMES_DEV, EPI, 128), BF16),
            pltpu.VMEM((FRAMES_DEV, ROWS, EPI), BF16),
            pltpu.VMEM((FRAMES_DEV, TOKENS, 128), BF16),
            pltpu.VMEM((FRAMES_DEV, TILES, ROWS, TILE), F32),
            pltpu.VMEM((FRAMES_DEV, TILES, 8, TILE), F32),
            pltpu.VMEM((TOKENS, TILE), F32),
            pltpu.VMEM((N, *block), BF16),
            pltpu.VMEM((N, *block), BF16),
            pltpu.SMEM((2 * N,), jnp.int32),
            pltpu.SMEM((FRAMES_DEV * ENTRIES,), jnp.int32),
            pltpu.SemaphoreType.DMA((2, N)),
            pltpu.SemaphoreType.DMA((2, N)),
            pltpu.SemaphoreType.DMA((2, N)),
            pltpu.SemaphoreType.DMA((2, N)),
            pltpu.SemaphoreType.DMA((2, 3)),
        ],
        compiler_params=pltpu.CompilerParams(
            collective_id=0, has_side_effects=True, vmem_limit_bytes=60 * 2**20
        ),
    )(queries, keys, values, epi_dev, epi_frame, epi_block, valid, ref_local)


def solution(mesh):
    shard = P("tm", "tok", None)
    return jax.shard_map(
        attention,
        mesh=mesh,
        in_specs=(shard, shard, shard, P(), P(), P(), P(), P()),
        out_specs=shard,
        check_vma=False,
    )
```

time: 328 us -> 84.7 us (0.26)
  the two profiles are of different devices: /device:TPU:24 before, /device:TPU:31 now
where the time goes in v1:
time: 84.7 us; the launch traced here: 84.4 us
  Pallas kernels  79.1 us (93%)
  local copies, waits for them, and re-layouts  5.32 us (6%)
    pallas_call x1, Pallas kernels, attention(): pl.pallas_call(kernel, out_shape=jax.ShapeDtypeStruct(queries.shape, BF16...  79.1 us
    unnamed x11, local copies, waits for them, and re-layouts  5.32 us

profile of v1, /device:TPU:31, one launch (start us, length us, event | category | flops | bytes accessed | tf_op | source)
XLA Modules:
  0.0 84.4 jit_solution(127841185745548375)
XLA Ops:
  0.0 0.0 copy-start
  0.0 1.4 %copy.9.dev_ref = s32[32,6]{1,0:T(8,128)} copy(s32[32,6]{0,1:T(8,128)} %param.11) | data formatting | bytes 1536 | tf_op args[3]
  1.4 0.0 copy-done
  1.4 0.0 copy-start.1
  1.4 0.7 copy.10.frame_ref
  2.1 0.0 copy-done.1
  2.1 0.0 copy-start.2
  2.1 0.7 copy.11.block_ref
  2.8 0.0 copy-done.2
  2.8 0.7 copy.12.valid_ref
  3.5 79.1 %shard_map.82 = bf16[2,128,1024]{2,1,0:T(8,128)(2,1)} custom-call(bf16[2,128,1024]{2,1,0:T(8,128)(2,1)} %q_ref.1, bf16[2,128,1024]{2,1,0:T(8,128)(2,1)} %k_ref.1, bf16[2,128,1024]{2,1,0:T(8,128)(2,1)} %v_ref.1, s32[32,6]{1,0:T(8,128)} %copy.9.dev_ref, s32[32,6]{1,0:T(8,128)} %copy.10.frame_ref, s32[32,6]{1,0:T(8,128)} %copy.11.block_ref, ...), custom_call_target="tpu_custom_call" | custom-call | tf_op jit(solution)/shard_map/pallas_call | solution.py:282
  82.5 1.9 %copy.14 = bf16[2,128,1024]{2,1,0:T(8,128)(2,1)} copy(bf16[2,128,1024]{2,1,0:T(8,128)(2,1)} %shard_map.82) | data formatting | bytes 1048576
Async XLA Ops:
  0.0 1.4 %copy-start = (s32[32,6]{0,1:T(8,128)S(1)}, s32[32,6]{0,1:T(8,128)}, u32[]{:S(2)}) copy-start(s32[32,6]{0,1:T(8,128)} %param.12) | copy-start | bytes 2308
  1.4 0.7 copy-start.1
  2.1 0.7 copy-start.2

commit v2 on v1

v2 whole, which is shorter than its diff:
```python
import functools
import math

import jax
import jax.numpy as jnp
from jax import lax
from jax.experimental import pallas as pl
from jax.experimental.pallas import tpu as pltpu
from jax.sharding import PartitionSpec as P

HEADS = 16
HEAD_DIM = 64
BLOCK = 128
FRAMES_DEV = 2
ENTRIES = 6
SPAN = 4
TOKENS = 2048
N = 16
TILE = 1024
CHUNK = 256
TILES = TOKENS // TILE
ROWS = HEAD_DIM + 16
EPI = ENTRIES * BLOCK
QK_SCALE = HEAD_DIM**-0.5 * math.log2(math.e)
MESH = pl.DeviceIdType.MESH
BF16 = jnp.bfloat16
F32 = jnp.float32


def low_halves(a, b):
    return jnp.concatenate([a[:, :HEAD_DIM], b[:, :HEAD_DIM]], axis=1)


def high_halves(a, b):
    return jnp.concatenate([a[:, HEAD_DIM:], b[:, HEAD_DIM:]], axis=1)


def kernel(
    q_ref, k_ref, v_ref, dev_ref, frame_ref, block_ref, valid_ref, local_ref, o_ref,
    s_k, s_v, s_q, s_ref, r_q, r_ref, s_epi_k, s_epi_v, r_epi_k, r_epi_v, s_out, r_out,
    both_k, both_v, cands, cross, r_cross, k_own, v_own, k_epi, v_epi, q_two, acc, top, scores, send_table, recv_table,
    sem_k, sem_v, sem_q, sem_ref, sem_epi_k, sem_epi_v, sem_out, sem_hop,
):
    tm, tok = lax.axis_index("tm"), lax.axis_index("tok")
    core, pair = lax.rem(tm, 2), lax.rem(tm // 2, 2)
    partner, across = tm + 1 - 2 * core, tm + 2 - 4 * pair
    group = tm // SPAN

    def other(me, step):
        return lax.rem(me + step, N)

    def rest(fn):
        lax.fori_loop(1, N, lambda step, _: (fn(step), 0)[1], 0)

    def copy(src, dst, sems, sent, got, axis, to):
        return pltpu.make_async_remote_copy(
            src_ref=src, dst_ref=dst, send_sem=sems.at[0, sent], recv_sem=sems.at[1, got],
            device_id={axis: to}, device_id_type=MESH,
        )

    class Exchange:
        def __init__(self, src, dst, sems, axis):
            self.src, self.dst, self.sems, self.axis = src, dst, sems, axis
            self.me = tm if axis == "tm" else tok

        def to(self, peer):
            return copy(self.src.at[peer], self.dst.at[self.me], self.sems, peer, self.me, self.axis, peer)

        def start(self):
            rest(lambda step: self.to(other(self.me, step)).start())

        def keep(self):
            self.dst[self.me] = self.src[self.me]

        def arrive(self):
            def one(step):
                peer = other(self.me, step)
                copy(self.src.at[peer], self.dst.at[peer], self.sems, peer, peer, self.axis, peer).wait_recv()

            rest(one)

        def drain(self):
            rest(lambda step: self.to(other(self.me, step)).wait_send())

    r_k, r_v = both_k.at[0], both_v.at[0]
    swap_k, swap_v = Exchange(s_k, r_k, sem_k, "tok"), Exchange(s_v, r_v, sem_v, "tok")
    swap_q, swap_ref = Exchange(s_q, r_q, sem_q, "tok"), Exchange(s_ref, r_ref, sem_ref, "tok")
    epi_k, epi_v = Exchange(s_epi_k, r_epi_k, sem_epi_k, "tm"), Exchange(s_epi_v, r_epi_v, sem_epi_v, "tm")
    outs = Exchange(s_out, r_out, sem_out, "tok")

    barrier = pltpu.get_barrier_semaphore()

    def greet(step):
        pl.semaphore_signal(barrier, inc=1, device_id={"tok": other(tok, step)}, device_id_type=MESH)
        pl.semaphore_signal(barrier, inc=1, device_id={"tm": other(tm, step)}, device_id_type=MESH)

    rest(greet)

    def pack(ref, out):
        for j in range(HEADS // 2):
            lanes = slice(j * 128, (j + 1) * 128)
            a, b = ref[0, :, lanes], ref[1, :, lanes]
            out[2 * j] = low_halves(a, b)
            out[2 * j + 1] = high_halves(a, b)

    pack(k_ref, s_k)
    pack(v_ref, s_v)
    pack(q_ref, s_q)
    local = local_ref[group]
    owner_core, owner_pair, ref_bit = lax.rem(local // 2, 2), local // 4, lax.rem(local, 2)
    for j in range(HEADS // 2):
        lanes = slice(j * 128, (j + 1) * 128)
        a, b = k_ref[ref_bit, :, lanes], v_ref[ref_bit, :, lanes]
        cands[core, 2 * j] = low_halves(a, b)
        cands[core, 2 * j + 1] = high_halves(a, b)

    pl.semaphore_wait(barrier, 2 * (N - 1))
    swap = copy(cands.at[core], cands.at[core], sem_hop, 0, 0, "tm", partner)
    swap.start()
    for exchange in (swap_k, swap_v, swap_q):
        exchange.start()
    for exchange in (swap_k, swap_v, swap_q):
        exchange.keep()

    part = N // 2
    mine, theirs = pl.ds(core * part, part), pl.ds((1 - core) * part, part)
    swap.wait_recv()
    cross[...] = cands[owner_core, mine]
    hop = copy(cross, r_cross.at[mine], sem_hop, 1, 1, "tm", across)
    hop.start()

    def fill_send(d, _):
        count, first, second = jnp.int32(0), jnp.int32(0), jnp.int32(0)
        for f in range(FRAMES_DEV):
            for e in range(ENTRIES):
                row = d * FRAMES_DEV + f
                hit = jnp.where(dev_ref[e, row] == tm, 1, 0)
                place = block_ref[e, row] * 2 + frame_ref[e, row]
                first = jnp.where((hit == 1) & (count == 0), place, first)
                second = jnp.where((hit == 1) & (count == 1), place, second)
                count = count + hit
        send_table[d * 2] = first
        send_table[d * 2 + 1] = second
        return 0

    lax.fori_loop(0, N, fill_send, 0)
    names = [dev_ref[e, tm * FRAMES_DEV + f] for f in range(FRAMES_DEV) for e in range(ENTRIES)]
    for i, name in enumerate(names):
        slot = jnp.int32(0)
        for before in names[:i]:
            slot = slot + jnp.where(before == name, 1, 0)
        recv_table[i] = name * 2 + jnp.minimum(slot, 1)

    acc[...] = jnp.zeros_like(acc)
    top[...] = jnp.full_like(top, -1e30)
    for f in range(3):
        v_own[f, 0:16, :] = jnp.ones((16, TOKENS), BF16)

    low = lax.broadcasted_iota(jnp.int32, (BLOCK, 128), 1) < HEAD_DIM

    def over_blocks(fn):
        def one(b, _):
            fn(b, pl.ds(pl.multiple_of(b * BLOCK, BLOCK), BLOCK))
            return 0

        lax.fori_loop(0, N, one, 0, unroll=4)

    def fill_epi(both, s_epi):
        def one(d, _):
            first, second = send_table[d * 2], send_table[d * 2 + 1]
            a, b = both[lax.rem(first, 2), first // 2], both[1 - lax.rem(second, 2), second // 2]
            s_epi[d] = jnp.where(low, a, b)
            return 0

        lax.fori_loop(0, N, one, 0, unroll=4)

    swap_k.arrive()

    def build_k(b, at):
        x = both_k[0, b]
        y = jnp.concatenate([x[:, HEAD_DIM:], x[:, :HEAD_DIM]], axis=1)
        both_k[1, b] = y
        k_own[0, at, :] = jnp.where(low, x, y)
        k_own[1, at, :] = jnp.where(low, y, x)

    over_blocks(build_k)
    fill_epi(both_k, s_epi_k)
    epi_k.start()
    epi_k.keep()

    hop.wait_recv()
    swap_back = copy(r_cross.at[mine], r_cross.at[mine], sem_hop, 2, 2, "tm", partner)
    swap_in = copy(r_cross.at[theirs], r_cross.at[theirs], sem_hop, 2, 2, "tm", partner)
    swap_back.start()

    swap_v.arrive()

    def build_v(b, at):
        x = both_v[0, b]
        both_v[1, b] = jnp.concatenate([x[:, HEAD_DIM:], x[:, :HEAD_DIM]], axis=1)
        x = x.T
        v_own[0, 16:, at] = x[:HEAD_DIM]
        v_own[1, 16:, at] = x[HEAD_DIM:]

    over_blocks(build_v)
    fill_epi(both_v, s_epi_v)
    epi_v.start()
    epi_v.keep()

    swap_in.wait_recv()

    def pick_ref(b, at):
        s_ref[b] = jnp.where(owner_pair == pair, cands[owner_core, b], r_cross[b])

    over_blocks(pick_ref)
    swap_ref.start()
    swap_ref.keep()

    swap_q.arrive()

    def build_q(b, at):
        x = r_q[b].astype(F32) * QK_SCALE
        hi = x.astype(BF16)
        lo = (x - hi.astype(F32)).astype(BF16)
        q_two[0, at, :] = low_halves(hi, lo)
        q_two[1, at, :] = high_halves(hi, lo)

    over_blocks(build_q)

    def attend(f, tile, keys, values):
        rows = pl.ds(pl.multiple_of(tile * TILE, TILE), TILE)
        parts = keys.shape[0] // CHUNK

        def score(c):
            s = lax.dot_general(
                keys[c * CHUNK:(c + 1) * CHUNK, :], q_two[f, rows, :], (((1,), (1,)), ((), ())),
                preferred_element_type=F32,
            )
            scores[c % 2] = s
            return jnp.max(s.reshape(CHUNK // 8, 8, TILE), axis=0)

        peak, old, total = score(0), top[f, tile], acc[f, tile]
        for c in range(parts):
            following = score(c + 1) if c + 1 < parts else None
            new = jnp.maximum(old, jnp.broadcast_to(jnp.max(peak, axis=0, keepdims=True), (8, TILE)))
            probs = jnp.exp2(scores[c % 2] - new[:1]).astype(BF16)
            part_sum = jnp.dot(values[:, c * CHUNK:(c + 1) * CHUNK], probs, preferred_element_type=F32)
            total = total * jnp.exp2(old - new)[:1] + part_sum
            old, peak = new, following
        top[f, tile] = old
        acc[f, tile] = total

    phase = FRAMES_DEV * TILES
    per_tile = TILE // BLOCK

    def build_ref(b, at):
        kv = r_ref[b]
        k_own[2, at, :] = low_halves(kv, kv)
        v_own[2, 16:, at] = kv.T[HEAD_DIM:]

    def half(x, bit):
        return jnp.where(bit == 0, x[:, :HEAD_DIM], x[:, HEAD_DIM:])

    def build_epi():
        for f in range(FRAMES_DEV):
            for e in range(ENTRIES):
                place = recv_table[f * ENTRIES + e]
                source, slot = place // 2, lax.rem(place, 2)
                used = valid_ref[e, tm * FRAMES_DEV + f] > 0
                x, stand_in = half(r_epi_k[source], slot), r_k[0][:, f * HEAD_DIM:(f + 1) * HEAD_DIM]
                x = jnp.where(used, x, stand_in)
                at = slice(e * BLOCK, (e + 1) * BLOCK)
                k_epi[f, at, :] = jnp.concatenate([x, x], axis=1)
                weight = jnp.where(used, 1.0, 0.0).astype(F32)
                v_epi[f, 0:16, at] = jnp.full((16, BLOCK), weight, F32).astype(BF16)
                y = r_epi_v[source]
                y = jnp.where(used, y, jnp.zeros_like(y)).T
                v_epi[f, 16:, at] = jnp.where(slot == 0, y[:HEAD_DIM], y[HEAD_DIM:])

    def long_step(n, _):
        @pl.when(n == phase)
        def _():
            swap_ref.arrive()
            over_blocks(build_ref)

        f, tile = lax.rem(n, FRAMES_DEV), lax.rem(n // FRAMES_DEV, TILES)
        which = jnp.where(n < phase, f, 2)
        attend(f, tile, k_own.at[which], v_own.at[which])
        return 0

    lax.fori_loop(0, 2 * phase, long_step, 0)
    epi_k.arrive()
    epi_v.arrive()
    build_epi()

    def short_step(n, _):
        f, tile = lax.rem(n, FRAMES_DEV), lax.rem(n // FRAMES_DEV + tok // per_tile, TILES)
        attend(f, tile, k_epi.at[f], v_epi.at[f])

        @pl.when(f == FRAMES_DEV - 1)
        def _():
            both = [acc[g, tile] for g in range(FRAMES_DEV)]
            both = [x[16:] / x[:1] for x in both]
            both = jnp.concatenate(both, axis=0).astype(BF16).T
            s_out[pl.ds(tile * per_tile, per_tile)] = both.reshape(per_tile, BLOCK, 128)
            for b in range(per_tile):
                to = tile * per_tile + b

                @pl.when(to != tok)
                def _():
                    outs.to(to).start()

        return 0

    lax.fori_loop(0, phase, short_step, 0)
    outs.keep()
    for exchange in (swap_k, swap_v, swap_q, swap_ref, epi_k, epi_v):
        exchange.drain()
    swap.wait_send()
    hop.wait_send()
    swap_back.wait_send()
    outs.arrive()
    for j in range(HEADS // 2):
        lanes = slice(j * 128, (j + 1) * 128)
        a, b = r_out[2 * j], r_out[2 * j + 1]
        o_ref[0, :, lanes] = low_halves(a, b)
        o_ref[1, :, lanes] = high_halves(a, b)
    outs.drain()


def attention(queries, keys, values, epi_dev, epi_frame, epi_block, valid, ref_local):
    vmem, smem = pl.BlockSpec(memory_space=pltpu.VMEM), pl.BlockSpec(memory_space=pltpu.SMEM)
    blocks = pltpu.VMEM((N, BLOCK, 128), BF16)
    tables = [x.T for x in (epi_dev, epi_frame, epi_block, valid)]
    return pl.pallas_call(
        kernel,
        out_shape=jax.ShapeDtypeStruct(queries.shape, BF16),
        in_specs=[vmem] * 3 + [smem] * 5,
        out_specs=vmem,
        scratch_shapes=[
            *[blocks] * 12,
            *[pltpu.VMEM((2, N, BLOCK, 128), BF16)] * 2,
            pltpu.VMEM((2, N, BLOCK, 128), BF16),
            pltpu.VMEM((N // 2, BLOCK, 128), BF16),
            blocks,
            pltpu.VMEM((3, TOKENS, 128), BF16),
            pltpu.VMEM((3, ROWS, TOKENS), BF16),
            pltpu.VMEM((FRAMES_DEV, EPI, 128), BF16),
            pltpu.VMEM((FRAMES_DEV, ROWS, EPI), BF16),
            pltpu.VMEM((FRAMES_DEV, TOKENS, 128), BF16),
            pltpu.VMEM((FRAMES_DEV, TILES, ROWS, TILE), F32),
            pltpu.VMEM((FRAMES_DEV, TILES, 8, TILE), F32),
            pltpu.VMEM((2, CHUNK, TILE), F32),
            pltpu.SMEM((2 * N,), jnp.int32),
            pltpu.SMEM((FRAMES_DEV * ENTRIES,), jnp.int32),
            *[pltpu.SemaphoreType.DMA((2, N))] * 7,
            pltpu.SemaphoreType.DMA((2, 3)),
        ],
        compiler_params=pltpu.CompilerParams(
            collective_id=0, has_side_effects=True, vmem_limit_bytes=60 * 2**20
        ),
    )(queries, keys, values, *tables, ref_local)


def solution(mesh):
    shard = P("tm", "tok", None)
    return jax.shard_map(
        attention,
        mesh=mesh,
        in_specs=(shard, shard, shard, P(), P(), P(), P(), P()),
        out_specs=shard,
        check_vma=False,
    )
```

time: 84.7 us -> 71.9 us (0.85)
  the two profiles are of different devices: /device:TPU:31 before, /device:TPU:24 now
where the time goes in v2:
time: 71.9 us; the launch traced here: 71.7 us
  Pallas kernels  69.8 us (97%)
  local copies, waits for them, and re-layouts  1.87 us (3%)
    pallas_call x1, Pallas kernels, attention(): pl.pallas_call(kernel, out_shape=jax.ShapeDtypeStruct(queries.shape, BF16...  69.8 us
    unnamed x1, local copies, waits for them, and re-layouts  1.87 us

profile of v2, /device:TPU:24, one launch (start us, length us, event | category | flops | bytes accessed | tf_op | source)
XLA Modules:
  0.0 71.7 jit_solution(4094037317956504168)
XLA Ops:
  0.0 69.8 %shard_map.82 = bf16[2,128,1024]{2,1,0:T(8,128)(2,1)} custom-call(bf16[2,128,1024]{2,1,0:T(8,128)(2,1)} %q_ref.1, bf16[2,128,1024]{2,1,0:T(8,128)(2,1)} %k_ref.1, bf16[2,128,1024]{2,1,0:T(8,128)(2,1)} %v_ref.1, s32[6,32]{1,0:T(8,128)} %bitcast.4, s32[6,32]{1,0:T(8,128)} %bitcast.5, s32[6,32]{1,0:T(8,128)} %bitcast.6, s32[6,32]{1,0:T(8,128)} %bitcast.7, ...), custom_call_target="tpu_custom_call" | custom-call | tf_op jit(solution)/shard_map/pallas_call | solution.py:335
  69.8 1.9 %copy.10 = bf16[2,128,1024]{2,1,0:T(8,128)(2,1)} copy(bf16[2,128,1024]{2,1,0:T(8,128)(2,1)} %shard_map.82) | data formatting | bytes 1048576

commit v3 on v2

--- a/solution.py
+++ b/solution.py
@@ -18,6 +18,8 @@
 N = 16
 TILE = 1024
 CHUNK = 256
+COLUMN = 256
+DEPTH = 8
 TILES = TOKENS // TILE
 ROWS = HEAD_DIM + 16
 EPI = ENTRIES * BLOCK
@@ -227,31 +229,30 @@
 
     over_blocks(build_q)
 
-    def attend(f, tile, keys, values):
-        rows = pl.ds(pl.multiple_of(tile * TILE, TILE), TILE)
-        parts = keys.shape[0] // CHUNK
-
-        def score(c):
+    def attend(work, keys, values):
+        def score(i):
+            f, column, c = work[i]
+            rows = pl.ds(pl.multiple_of(column * COLUMN, COLUMN), COLUMN)
             s = lax.dot_general(
-                keys[c * CHUNK:(c + 1) * CHUNK, :], q_two[f, rows, :], (((1,), (1,)), ((), ())),
+                keys(f)[c * CHUNK:(c + 1) * CHUNK, :], q_two[f, rows, :], (((1,), (1,)), ((), ())),
                 preferred_element_type=F32,
             )
-            scores[c % 2] = s
-            return jnp.max(s.reshape(CHUNK // 8, 8, TILE), axis=0)
-
-        peak, old, total = score(0), top[f, tile], acc[f, tile]
-        for c in range(parts):
-            following = score(c + 1) if c + 1 < parts else None
-            new = jnp.maximum(old, jnp.broadcast_to(jnp.max(peak, axis=0, keepdims=True), (8, TILE)))
-            probs = jnp.exp2(scores[c % 2] - new[:1]).astype(BF16)
-            part_sum = jnp.dot(values[:, c * CHUNK:(c + 1) * CHUNK], probs, preferred_element_type=F32)
-            total = total * jnp.exp2(old - new)[:1] + part_sum
-            old, peak = new, following
-        top[f, tile] = old
-        acc[f, tile] = total
-
-    phase = FRAMES_DEV * TILES
-    per_tile = TILE // BLOCK
+            scores[i % (DEPTH + 1)] = s
+            return jnp.max(s.reshape(CHUNK // 8, 8, COLUMN), axis=0)
+
+        peaks = {i: score(i) for i in range(DEPTH)}
+        for i, (f, column, c) in enumerate(work):
+            if i + DEPTH < len(work):
+                peaks[i + DEPTH] = score(i + DEPTH)
+            old = top[f, column]
+            peak = jnp.max(peaks.pop(i), axis=0, keepdims=True)
+            new = jnp.maximum(old, jnp.broadcast_to(peak, (8, COLUMN)))
+            probs = jnp.exp2(scores[i % (DEPTH + 1)] - new[:1]).astype(BF16)
+            part_sum = jnp.dot(values(f)[:, c * CHUNK:(c + 1) * CHUNK], probs, preferred_element_type=F32)
+            acc[f, column] = acc[f, column] * jnp.exp2(old - new)[:1] + part_sum
+            top[f, column] = new
+
+    per_tile, columns = TILE // BLOCK, TILE // COLUMN
 
     def build_ref(b, at):
         kv = r_ref[b]
@@ -278,41 +279,42 @@
                 v_epi[f, 16:, at] = jnp.where(slot == 0, y[:HEAD_DIM], y[HEAD_DIM:])
 
     def long_step(n, _):
-        @pl.when(n == phase)
+        @pl.when(n == FRAMES_DEV)
         def _():
             swap_ref.arrive()
             over_blocks(build_ref)
 
-        f, tile = lax.rem(n, FRAMES_DEV), lax.rem(n // FRAMES_DEV, TILES)
-        which = jnp.where(n < phase, f, 2)
-        attend(f, tile, k_own.at[which], v_own.at[which])
+        which = jnp.where(n < FRAMES_DEV, n, 2)
+        work = [(lax.rem(n, FRAMES_DEV), t, c) for c in range(TOKENS // CHUNK) for t in range(TOKENS // COLUMN)]
+        attend(work, lambda f: k_own.at[which], lambda f: v_own.at[which])
         return 0
 
-    lax.fori_loop(0, 2 * phase, long_step, 0)
+    lax.fori_loop(0, 2 * FRAMES_DEV, long_step, 0)
     epi_k.arrive()
     epi_v.arrive()
     build_epi()
 
     def short_step(n, _):
-        f, tile = lax.rem(n, FRAMES_DEV), lax.rem(n // FRAMES_DEV + tok // per_tile, TILES)
-        attend(f, tile, k_epi.at[f], v_epi.at[f])
-
-        @pl.when(f == FRAMES_DEV - 1)
-        def _():
-            both = [acc[g, tile] for g in range(FRAMES_DEV)]
-            both = [x[16:] / x[:1] for x in both]
-            both = jnp.concatenate(both, axis=0).astype(BF16).T
-            s_out[pl.ds(tile * per_tile, per_tile)] = both.reshape(per_tile, BLOCK, 128)
-            for b in range(per_tile):
-                to = tile * per_tile + b
-
-                @pl.when(to != tok)
-                def _():
-                    outs.to(to).start()
+        tile = lax.rem(n + tok // per_tile, TILES)
+        work = [
+            (f, tile * columns + t, c)
+            for f in range(FRAMES_DEV) for c in range(EPI // CHUNK) for t in range(columns)
+        ]
+        attend(work, lambda f: k_epi.at[f], lambda f: v_epi.at[f])
+        for t in range(columns):
+            both = [acc[f, tile * columns + t] for f in range(FRAMES_DEV)]
+            both = jnp.concatenate([x[16:] / x[:1] for x in both], axis=0).astype(BF16).T
+            s_out[pl.ds(tile * per_tile + t * (COLUMN // BLOCK), COLUMN // BLOCK)] = both.reshape(-1, BLOCK, 128)
+        for b in range(per_tile):
+            to = tile * per_tile + b
+
+            @pl.when(to != tok)
+            def _():
+                outs.to(to).start()
 
         return 0
 
-    lax.fori_loop(0, phase, short_step, 0)
+    lax.fori_loop(0, TILES, short_step, 0)
     outs.keep()
     for exchange in (swap_k, swap_v, swap_q, swap_ref, epi_k, epi_v):
         exchange.drain()
@@ -348,9 +350,9 @@
             pltpu.VMEM((FRAMES_DEV, EPI, 128), BF16),
             pltpu.VMEM((FRAMES_DEV, ROWS, EPI), BF16),
             pltpu.VMEM((FRAMES_DEV, TOKENS, 128), BF16),
-            pltpu.VMEM((FRAMES_DEV, TILES, ROWS, TILE), F32),
-            pltpu.VMEM((FRAMES_DEV, TILES, 8, TILE), F32),
-            pltpu.VMEM((2, CHUNK, TILE), F32),
+            pltpu.VMEM((FRAMES_DEV, TOKENS // COLUMN, ROWS, COLUMN), F32),
+            pltpu.VMEM((FRAMES_DEV, TOKENS // COLUMN, 8, COLUMN), F32),
+            pltpu.VMEM((DEPTH + 1, CHUNK, COLUMN), F32),
             pltpu.SMEM((2 * N,), jnp.int32),
             pltpu.SMEM((FRAMES_DEV * ENTRIES,), jnp.int32),
             *[pltpu.SemaphoreType.DMA((2, N))] * 7,

time: 71.9 us -> 67.6 us (0.940)
  Pallas kernels: 69.8 us -> 65.4 us
    pallas_call x1, Pallas kernels: 69.8 us -> 65.4 us  [attention(): pl.pallas_call(kernel, out_shape=jax.ShapeDtypeStruct(queries.shape, BF16...]
where the time goes in v3:
time: 67.6 us; the launch traced here: 67.3 us
  Pallas kernels  65.4 us (97%)
  local copies, waits for them, and re-layouts  1.87 us (3%)
    pallas_call x1, Pallas kernels, attention(): pl.pallas_call(kernel, out_shape=jax.ShapeDtypeStruct(queries.shape, BF16...  65.4 us
    unnamed x1, local copies, waits for them, and re-layouts  1.87 us

profile of v3, /device:TPU:24, one launch (start us, length us, event | category | flops | bytes accessed | tf_op | source)
XLA Modules:
  0.0 67.3 jit_solution(5879335294077292168)
XLA Ops:
  0.0 65.4 %shard_map.82 = bf16[2,128,1024]{2,1,0:T(8,128)(2,1)} custom-call(bf16[2,128,1024]{2,1,0:T(8,128)(2,1)} %q_ref.1, bf16[2,128,1024]{2,1,0:T(8,128)(2,1)} %k_ref.1, bf16[2,128,1024]{2,1,0:T(8,128)(2,1)} %v_ref.1, s32[6,32]{1,0:T(8,128)} %bitcast.4, s32[6,32]{1,0:T(8,128)} %bitcast.5, s32[6,32]{1,0:T(8,128)} %bitcast.6, s32[6,32]{1,0:T(8,128)} %bitcast.7, ...), custom_call_target="tpu_custom_call" | custom-call | tf_op jit(solution)/shard_map/pallas_call | solution.py:337
  65.4 1.9 %copy.10 = bf16[2,128,1024]{2,1,0:T(8,128)(2,1)} copy(bf16[2,128,1024]{2,1,0:T(8,128)(2,1)} %shard_map.82) | data formatting | bytes 1048576

commit v4 on v3

--- a/solution.py
+++ b/solution.py
@@ -38,10 +38,10 @@
 
 
 def kernel(
-    q_ref, k_ref, v_ref, dev_ref, frame_ref, block_ref, valid_ref, local_ref, o_ref,
-    s_k, s_v, s_q, s_ref, r_q, r_ref, s_epi_k, s_epi_v, r_epi_k, r_epi_v, s_out, r_out,
-    both_k, both_v, cands, cross, r_cross, k_own, v_own, k_epi, v_epi, q_two, acc, top, scores, send_table, recv_table,
-    sem_k, sem_v, sem_q, sem_ref, sem_epi_k, sem_epi_v, sem_out, sem_hop,
+    q_hbm, k_hbm, v_hbm, dev_ref, frame_ref, block_ref, valid_ref, local_ref, o_ref,
+    q_ref, k_ref, v_ref, s_k, s_v, s_q, s_ref, r_q, r_ref, s_epi_k, s_epi_v, r_epi_k, r_epi_v, s_out, r_out,
+    both_k, both_v, cands, cross, r_cross, k_own, v_own, k_epi, v_epi, q_two, acc, top, scores, send_table,
+    sem_k, sem_v, sem_q, sem_ref, sem_epi_k, sem_epi_v, sem_out, sem_hop, sem_in,
 ):
     tm, tok = lax.axis_index("tm"), lax.axis_index("tok")
     core, pair = lax.rem(tm, 2), lax.rem(tm // 2, 2)
@@ -96,6 +96,12 @@
         pl.semaphore_signal(barrier, inc=1, device_id={"tok": other(tok, step)}, device_id_type=MESH)
         pl.semaphore_signal(barrier, inc=1, device_id={"tm": other(tm, step)}, device_id_type=MESH)
 
+    fetches = [
+        pltpu.make_async_copy(src, dst, sem_in.at[i])
+        for i, (src, dst) in enumerate(((k_hbm, k_ref), (v_hbm, v_ref), (q_hbm, q_ref)))
+    ]
+    for fetch in fetches:
+        fetch.start()
     rest(greet)
 
     def pack(ref, out):
@@ -105,9 +111,9 @@
             out[2 * j] = low_halves(a, b)
             out[2 * j + 1] = high_halves(a, b)
 
-    pack(k_ref, s_k)
-    pack(v_ref, s_v)
-    pack(q_ref, s_q)
+    for fetch, ref, out in zip(fetches, (k_ref, v_ref, q_ref), (s_k, s_v, s_q)):
+        fetch.wait()
+        pack(ref, out)
     local = local_ref[group]
     owner_core, owner_pair, ref_bit = lax.rem(local // 2, 2), local // 4, lax.rem(local, 2)
     for j in range(HEADS // 2):
@@ -132,26 +138,15 @@
     hop.start()
 
     def fill_send(d, _):
-        count, first, second = jnp.int32(0), jnp.int32(0), jnp.int32(0)
         for f in range(FRAMES_DEV):
+            row, place = d * FRAMES_DEV + f, jnp.int32(0)
             for e in range(ENTRIES):
-                row = d * FRAMES_DEV + f
-                hit = jnp.where(dev_ref[e, row] == tm, 1, 0)
-                place = block_ref[e, row] * 2 + frame_ref[e, row]
-                first = jnp.where((hit == 1) & (count == 0), place, first)
-                second = jnp.where((hit == 1) & (count == 1), place, second)
-                count = count + hit
-        send_table[d * 2] = first
-        send_table[d * 2 + 1] = second
+                spot = block_ref[e, row] * 2 + frame_ref[e, row]
+                place = jnp.where(dev_ref[e, row] == tm, spot, place)
+            send_table[d * 2 + f] = place
         return 0
 
     lax.fori_loop(0, N, fill_send, 0)
-    names = [dev_ref[e, tm * FRAMES_DEV + f] for f in range(FRAMES_DEV) for e in range(ENTRIES)]
-    for i, name in enumerate(names):
-        slot = jnp.int32(0)
-        for before in names[:i]:
-            slot = slot + jnp.where(before == name, 1, 0)
-        recv_table[i] = name * 2 + jnp.minimum(slot, 1)
 
     acc[...] = jnp.zeros_like(acc)
     top[...] = jnp.full_like(top, -1e30)
@@ -259,24 +254,18 @@
         k_own[2, at, :] = low_halves(kv, kv)
         v_own[2, 16:, at] = kv.T[HEAD_DIM:]
 
-    def half(x, bit):
-        return jnp.where(bit == 0, x[:, :HEAD_DIM], x[:, HEAD_DIM:])
-
     def build_epi():
         for f in range(FRAMES_DEV):
+            side = slice(f * HEAD_DIM, (f + 1) * HEAD_DIM)
             for e in range(ENTRIES):
-                place = recv_table[f * ENTRIES + e]
-                source, slot = place // 2, lax.rem(place, 2)
-                used = valid_ref[e, tm * FRAMES_DEV + f] > 0
-                x, stand_in = half(r_epi_k[source], slot), r_k[0][:, f * HEAD_DIM:(f + 1) * HEAD_DIM]
-                x = jnp.where(used, x, stand_in)
-                at = slice(e * BLOCK, (e + 1) * BLOCK)
+                row, at = tm * FRAMES_DEV + f, slice(e * BLOCK, (e + 1) * BLOCK)
+                source, used = dev_ref[e, row], valid_ref[e, row] > 0
+                x = jnp.where(used, r_epi_k[source][:, side], r_k[0][:, side])
                 k_epi[f, at, :] = jnp.concatenate([x, x], axis=1)
                 weight = jnp.where(used, 1.0, 0.0).astype(F32)
                 v_epi[f, 0:16, at] = jnp.full((16, BLOCK), weight, F32).astype(BF16)
                 y = r_epi_v[source]
-                y = jnp.where(used, y, jnp.zeros_like(y)).T
-                v_epi[f, 16:, at] = jnp.where(slot == 0, y[:HEAD_DIM], y[HEAD_DIM:])
+                v_epi[f, 16:, at] = jnp.where(used, y, jnp.zeros_like(y)).T[side]
 
     def long_step(n, _):
         @pl.when(n == FRAMES_DEV)
@@ -337,9 +326,10 @@
     return pl.pallas_call(
         kernel,
         out_shape=jax.ShapeDtypeStruct(queries.shape, BF16),
-        in_specs=[vmem] * 3 + [smem] * 5,
+        in_specs=[pl.BlockSpec(memory_space=pl.ANY)] * 3 + [smem] * 5,
         out_specs=vmem,
         scratch_shapes=[
+            *[pltpu.VMEM(queries.shape, BF16)] * 3,
             *[blocks] * 12,
             *[pltpu.VMEM((2, N, BLOCK, 128), BF16)] * 2,
             pltpu.VMEM((2, N, BLOCK, 128), BF16),
@@ -354,9 +344,9 @@
             pltpu.VMEM((FRAMES_DEV, TOKENS // COLUMN, 8, COLUMN), F32),
             pltpu.VMEM((DEPTH + 1, CHUNK, COLUMN), F32),
             pltpu.SMEM((2 * N,), jnp.int32),
-            pltpu.SMEM((FRAMES_DEV * ENTRIES,), jnp.int32),
             *[pltpu.SemaphoreType.DMA((2, N))] * 7,
             pltpu.SemaphoreType.DMA((2, 3)),
+            pltpu.SemaphoreType.DMA((3,)),
         ],
         compiler_params=pltpu.CompilerParams(
             collective_id=0, has_side_effects=True, vmem_limit_bytes=60 * 2**20

time: 67.6 us -> 65.9 us (0.975)
  Pallas kernels: 65.4 us -> 63.8 us
    pallas_call x1, Pallas kernels: 65.4 us -> 63.8 us  [attention(): pl.pallas_call(kernel, out_shape=jax.ShapeDtypeStruct(queries.shape, BF16...]
where the time goes in v4:
time: 65.9 us; the launch traced here: 65.6 us
  Pallas kernels  63.8 us (97%)
  local copies, waits for them, and re-layouts  1.87 us (3%)
    pallas_call x1, Pallas kernels, attention(): pl.pallas_call(kernel, out_shape=jax.ShapeDtypeStruct(queries.shape, BF16...  63.8 us
    unnamed x1, local copies, waits for them, and re-layouts  1.87 us

profile of v4, /device:TPU:24, one launch (start us, length us, event | category | flops | bytes accessed | tf_op | source)
XLA Modules:
  0.0 65.6 jit_solution(2538159759926440550)
XLA Ops:
  0.0 63.8 %shard_map.82 = bf16[2,128,1024]{2,1,0:T(8,128)(2,1)} custom-call(bf16[2,128,1024]{2,1,0:T(8,128)(2,1)} %q_hbm.1, bf16[2,128,1024]{2,1,0:T(8,128)(2,1)} %k_hbm.1, bf16[2,128,1024]{2,1,0:T(8,128)(2,1)} %v_hbm.1, s32[6,32]{1,0:T(8,128)} %bitcast.4, s32[6,32]{1,0:T(8,128)} %bitcast.5, s32[6,32]{1,0:T(8,128)} %bitcast.6, s32[6,32]{1,0:T(8,128)} %bitcast.7, ...), custom_call_target="tpu_custom_call" | custom-call | tf_op jit(solution)/shard_map/pallas_call | solution.py:326
  63.8 1.9 %copy.10 = bf16[2,128,1024]{2,1,0:T(8,128)(2,1)} copy(bf16[2,128,1024]{2,1,0:T(8,128)(2,1)} %shard_map.82) | data formatting | bytes 1048576

commit v5 on v4

--- a/solution.py
+++ b/solution.py
@@ -25,6 +25,11 @@
 EPI = ENTRIES * BLOCK
 QK_SCALE = HEAD_DIM**-0.5 * math.log2(math.e)
 MESH = pl.DeviceIdType.MESH
+SIDE = 4
+FAR_FIRST = sorted(
+    ((dx, dy) for dx in range(SIDE) for dy in range(SIDE) if dx or dy),
+    key=lambda d: -(min(d[0], SIDE - d[0]) + min(d[1], SIDE - d[1])),
+)
 BF16 = jnp.bfloat16
 F32 = jnp.float32
 
@@ -69,7 +74,12 @@
             return copy(self.src.at[peer], self.dst.at[self.me], self.sems, peer, self.me, self.axis, peer)
 
         def start(self):
-            rest(lambda step: self.to(other(self.me, step)).start())
+            if self.axis == "tm":
+                rest(lambda step: self.to(other(self.me, step)).start())
+                return
+            row, column = self.me // SIDE, lax.rem(self.me, SIDE)
+            for dx, dy in FAR_FIRST:
+                self.to(lax.rem(row + dx, SIDE) * SIDE + lax.rem(column + dy, SIDE)).start()
 
         def keep(self):
             self.dst[self.me] = self.src[self.me]
@@ -268,17 +278,23 @@
                 v_epi[f, 16:, at] = jnp.where(used, y, jnp.zeros_like(y)).T[side]
 
     def long_step(n, _):
-        @pl.when(n == FRAMES_DEV)
+        @pl.when(n == 1)
         def _():
             swap_ref.arrive()
             over_blocks(build_ref)
 
-        which = jnp.where(n < FRAMES_DEV, n, 2)
-        work = [(lax.rem(n, FRAMES_DEV), t, c) for c in range(TOKENS // CHUNK) for t in range(TOKENS // COLUMN)]
-        attend(work, lambda f: k_own.at[which], lambda f: v_own.at[which])
+        work = [
+            (f, t, c)
+            for f in range(FRAMES_DEV) for c in range(TOKENS // CHUNK) for t in range(TOKENS // COLUMN)
+        ]
+
+        def which(f):
+            return jnp.where(n == 0, f, FRAMES_DEV)
+
+        attend(work, lambda f: k_own.at[which(f)], lambda f: v_own.at[which(f)])
         return 0
 
-    lax.fori_loop(0, 2 * FRAMES_DEV, long_step, 0)
+    lax.fori_loop(0, 2, long_step, 0)
     epi_k.arrive()
     epi_v.arrive()
     build_epi()

time: 65.9 us -> 65.2 us (0.989)
  no operation moved by 1% of the time
where the time goes in v5:
time: 65.2 us; the launch traced here: 65.1 us
  Pallas kernels  63.2 us (97%)
  local copies, waits for them, and re-layouts  1.87 us (3%)
    pallas_call x1, Pallas kernels, attention(): pl.pallas_call(kernel, out_shape=jax.ShapeDtypeStruct(queries.shape, BF16...  63.2 us
    unnamed x1, local copies, waits for them, and re-layouts  1.87 us

profile of v5, /device:TPU:24, one launch (start us, length us, event | category | flops | bytes accessed | tf_op | source)
XLA Modules:
  0.0 65.1 jit_solution(2779583644562003322)
XLA Ops:
  0.0 63.2 %shard_map.82 = bf16[2,128,1024]{2,1,0:T(8,128)(2,1)} custom-call(bf16[2,128,1024]{2,1,0:T(8,128)(2,1)} %q_hbm.1, bf16[2,128,1024]{2,1,0:T(8,128)(2,1)} %k_hbm.1, bf16[2,128,1024]{2,1,0:T(8,128)(2,1)} %v_hbm.1, s32[6,32]{1,0:T(8,128)} %bitcast.4, s32[6,32]{1,0:T(8,128)} %bitcast.5, s32[6,32]{1,0:T(8,128)} %bitcast.6, s32[6,32]{1,0:T(8,128)} %bitcast.7, ...), custom_call_target="tpu_custom_call" | custom-call | tf_op jit(solution)/shard_map/pallas_call | solution.py:342
  63.2 1.9 %copy.10 = bf16[2,128,1024]{2,1,0:T(8,128)(2,1)} copy(bf16[2,128,1024]{2,1,0:T(8,128)(2,1)} %shard_map.82) | data formatting | bytes 1048576
